TPU v7x, 32 devices: a whole 2x2x4 slice. The times are simulated.
32 devices in a mesh: ctx: 8 (over z, x), tp: 4 (over y, core).
Axes of the slice: x: 2, y: 2, z: 4, core: 2. Of those that a mesh axis runs over, the one named last changes fastest.
Arguments:
- q_nope: bfloat16 [8, 128, 128], P('ctx', 'tp'), may hold values from -6 to 6
- q_rope: bfloat16 [8, 128, 64], P('ctx', 'tp'), may hold values from -256 to 256
- w_uk: bfloat16 [128, 128, 512], P('tp'), may hold values from -0.5 to 0.5
- w_uv: bfloat16 [128, 512, 128], P('tp'), may hold values from -3 to 3
- w_out: bfloat16 [16384, 7168], P('tp', 'ctx'), may hold values from -0.046875 to 0.046875
- prefix_cache: bfloat16 [32768, 576], P('ctx'), may hold values from -6 to 6
- block_table: int32 [512], P('ctx'), may hold values from 0 to 511, each once
- prefix_len: int32 [8], replicated, may hold values from 8192 to 32768
- suffix_cache: bfloat16 [8, 256, 576], P('ctx'), may hold values from -12 to 12
- suffix_len: int32 [8], P('ctx'), may hold values from 2 to 256
Outputs:
- layer_out: bfloat16 [8, 7168], P('tp', 'ctx')
Inputs may be any that keep to these rules, and one draw needn't show every extreme that they name: A permutation: slots b * 64 to b * 64 + 63 of prefix_cache hold prefix positions block_table[b] * 64 onwards.
All inputs are finite; a program needn't handle non-finite values.
Results may differ from a plain program's by a relative error of at most 0.0078.
Values may be sent and summed in bfloat16 or wider, within the bound.
A program may use at most 64 MiB of HBM per device.

v0:
```python
import jax
import jax.numpy as jnp
from jax import lax
from jax.sharding import PartitionSpec as P

LAT = 512
ROPE = 64
NOPE = 128
BLOCK = 64
masked_value = -1e30


def partial_stats(scores, visible, values, pattern):
    row_peak = jnp.max(jnp.where(visible, scores, masked_value), axis=2)
    weights = jnp.where(visible, jnp.exp(scores - row_peak[:, :, None]), 0.0).astype(jnp.bfloat16)
    row_mass = jnp.sum(weights, axis=2, dtype=jnp.float32)
    row_weighted = jnp.einsum(pattern, weights, values, preferred_element_type=jnp.float32)
    return (row_peak, row_mass, row_weighted)


def value_project(latent, value_weight):
    return jnp.einsum("rhc,hcv->rhv", latent, value_weight, precision=lax.Precision.HIGHEST)


def on_device(
    q_nope,
    q_rope,
    w_uk,
    w_uv,
    w_out,
    prefix_cache,
    block_table,
    prefix_len,
    suffix_cache,
    suffix_len,
):
    softmax_scale = (NOPE + ROPE) ** (-0.5)
    q_latent = jnp.einsum("rhn,hnc->rhc", q_nope, w_uk, preferred_element_type=jnp.float32).astype(
        jnp.bfloat16
    )
    own_queries = jnp.concatenate([q_latent, q_rope], axis=2)
    all_queries = lax.all_gather(own_queries, "ctx", axis=0, tiled=True)
    ctx_count = lax.axis_size("ctx")
    own_count = own_queries.shape[0]
    value_weight = w_uv.astype(jnp.float32)
    positions = (
        block_table[:, None] * BLOCK + jnp.arange(BLOCK, dtype=jnp.int32)[None, :]
    ).reshape(-1)
    visible = (positions[None, :] < prefix_len[:, None])[:, None, :]
    scores = (
        jnp.einsum("rhc,tc->rht", all_queries, prefix_cache, preferred_element_type=jnp.float32)
        * softmax_scale
    )
    row_peak, row_mass, row_weighted = partial_stats(
        scores, visible, prefix_cache[:, :LAT], "rht,tc->rhc"
    )
    suffix_scores = (
        jnp.einsum("rhc,rtc->rht", own_queries, suffix_cache, preferred_element_type=jnp.float32)
        * softmax_scale
    )
    suffix_slots = jnp.arange(suffix_cache.shape[1], dtype=jnp.int32)
    suffix_visible = (suffix_slots[None, :] < suffix_len[:, None])[:, None, :]
    tail_peak, tail_mass, tail_weighted = partial_stats(
        suffix_scores, suffix_visible, suffix_cache[:, :, :LAT], "rht,rtc->rhc"
    )

    def by_owner(values):
        return values.reshape((ctx_count, own_count) + values.shape[1:])

    got_peak, got_mass, got_weighted = (
        lax.all_to_all(by_owner(row_peak), "ctx", split_axis=0, concat_axis=0, tiled=True),
        lax.all_to_all(by_owner(row_mass), "ctx", split_axis=0, concat_axis=0, tiled=True),
        lax.all_to_all(by_owner(row_weighted), "ctx", split_axis=0, concat_axis=0, tiled=True),
    )
    highest = jnp.maximum(jnp.max(got_peak, axis=0), tail_peak)
    factors = jnp.exp(got_peak - highest[None])
    tail_factor = jnp.exp(tail_peak - highest)
    total_mass = jnp.sum(factors * got_mass, axis=0) + tail_factor * tail_mass
    total_weighted = (
        jnp.sum(factors[..., None] * got_weighted, axis=0) + tail_factor[:, :, None] * tail_weighted
    )
    head_values = value_project(total_weighted / total_mass[:, :, None], value_weight).astype(
        jnp.bfloat16
    )
    flat_values = head_values.reshape(own_count, -1)
    every_value = lax.all_gather(flat_values, "ctx", axis=0, tiled=True)
    return lax.psum_scatter(
        jnp.dot(every_value, w_out, preferred_element_type=jnp.float32),
        "tp",
        scatter_dimension=0,
        tiled=True,
    ).astype(jnp.bfloat16)


def solution(mesh):
    placed = (
        P("ctx", "tp", None),
        P("ctx", "tp", None),
        P("tp", None, None),
        P("tp", None, None),
        P("tp", "ctx"),
        P("ctx", None),
        P("ctx"),
        P(),
        P("ctx", None, None),
        P("ctx"),
    )
    return jax.shard_map(
        on_device, mesh=mesh, in_specs=placed, out_specs=P("tp", "ctx"), check_vma=False
    )
```

profile of v0, /device:TPU:0, one launch (start us, length us, event | category | flops | bytes accessed | tf_op | source)
XLA Modules:
  0.0 129.5 jit_solution(10840114998855403633)
XLA Ops:
  0.0 0.0 copy-start
  0.0 0.0 copy-start.3
  0.0 0.0 copy-start.4
  0.0 0.7 broadcast_multiply_fusion
  0.7 0.1 iota_add_fusion
  0.8 0.1 add.38
  0.9 0.0 copy-done
  0.9 0.0 copy-start.5
  0.9 3.0 %fusion.20 = bf16[32,1,512]{2,1,0:T(2,128)(2,1)S(1)} fusion(bf16[32,128,512]{2,1,0:T(8,128)(2,1)} %param.12, bf16[32,128,1]{1,0,2:T(8,128)(2,1)S(1)} %bitcast.55), kind=kOutput, calls=%fused_computation.32 | convolution fusion | flops 4194304 | bytes 4235264 | tf_op jit(solution)/shard_map/rhn,hnc->rhc/dot_general | solution.py:38
  3.9 0.0 copy-done.3
  3.9 32.7 %all_gather.6 = bf16[8,32,576]{2,1,0:T(8,128)(2,1)S(1)} all-gather(bf16[1,32,576]{2,1,0:T(8,128)(2,1)S(1)} %pad_maximum_fusion), channel_id=1, replica_groups=mesh['ctx'=8,'tp'=4] {'ctx'}, dimensions={0}, use_global_device_ids=true | all-gather | bytes 331776 | tf_op jit(solution)/shard_map/all_gather | solution.py:42
  36.6 0.0 copy-done.4
  36.6 0.1 broadcast_compare_fusion
  36.7 0.0 copy-done.5
  36.7 2.7 %select_reduce_fusion = (f32[8,32]{1,0:T(8,128)}, f32[8,32,4096]{2,1,0:T(8,128)S(1)}) fusion(pred[8,4096]{1,0:T(8,128)(4,1)S(1)} %broadcast_compare_fusion, bf16[8,32,576]{2,1,0:T(8,128)(2,1)S(1)} %all_gather.6, bf16[4096,576]{0,1:T(8,128)(2,1)S(1)} %copy-done.5), kind=kOutput, calls=%fused_computation.7 | convolution fusion | flops 1211105024 | bytes 9241600 | tf_op jit(solution)/shard_map/rhc,tc->rht/dot_general | solution.py:51
  39.4 0.0 copy-start.1
  39.4 1.9 %copy-done.1 = f32[8,32,4096]{2,1,0:T(8,128)} copy-done((f32[8,32,4096]{2,1,0:T(8,128)}, f32[8,32,4096]{2,1,0:T(8,128)S(1)}, u32[]{:S(2)}) %copy-start.1) | copy-done | bytes 4194328
  41.3 1.7 %convert_reduce_fusion = f32[8,32]{1,0:T(8,128)S(1)} fusion(f32[8,32,4096]{2,1,0:T(8,128)S(1)} %get-tuple-element.10, f32[8,32]{1,0:T(8,128)} %get-tuple-element.9, pred[8,4096]{1,0:T(8,128)(4,1)S(1)} %broadcast_compare_fusion), kind=kLoop, calls=%fused_computation.4 | loop fusion | flops 5242624 | bytes 4229120 | tf_op jit(solution)/shard_map/reduce_sum | solution.py:16
  43.0 11.8 %all_to_all.15 = f32[8,1,32]{2,1,0:T(1,128)S(1)} all-to-all(f32[8,1,32]{2,1,0:T(1,128)S(1)} %bitcast.60), channel_id=1, replica_groups=mesh['ctx'=8,'tp'=4] {'ctx'}, dimensions={0} | all-to-all | bytes 2048 | tf_op jit(solution)/shard_map/all_to_all | solution.py:72
  54.9 3.2 %all-to-all-start = ((f32[8,1,32]{2,1,0:T(1,128)}), f32[8,1,32]{2,1,0:T(1,128)S(1)}, u32[]{:S(2)}, u32[]{:S(2)}) async-start(f32[8,1,32]{2,1,0:T(1,128)} %bitcast.5), calls=%async_computation | async-start | bytes 8192 | tf_op jit(solution)/shard_map/all_to_all | solution.py:71
  58.1 0.0 copy-start.6
  58.1 0.0 copy-start.2
  58.1 5.6 %fusion.4 = f32[8,1,32,512]{3,2,1,0:T(8,128)} fusion(bf16[4096,576]{0,1:T(8,128)(2,1)} %param.15, f32[8,32,4096]{2,1,0:T(8,128)} %copy-done.1, f32[8,32]{1,0:T(8,128)} %get-tuple-element.9, pred[8,4096]{1,0:T(8,128)(4,1)S(1)} %broadcast_compare_fusion), kind=kOutput, calls=%fused_computation.8 | convolution fusion | flops 1076887552 | bytes 8949760 | tf_op jit(solution)/shard_map/rht,tc->rhc/dot_general | solution.py:17
  63.7 0.8 all-to-all-done
  64.5 5.1 %all-to-all-start.1 = ((f32[8,1,32,512]{3,2,1,0:T(8,128)}), f32[8,1,32,512]{3,2,1,0:T(8,128)S(1)}, u32[]{:S(2)}, u32[]{:S(2)}) async-start(f32[8,1,32,512]{3,2,1,0:T(8,128)} %fusion.4), calls=%async_computation.1 | async-start | bytes 1048576 | tf_op jit(solution)/shard_map/all_to_all | solution.py:73
  70.3 0.0 copy-done.6
  70.3 0.7 dynamic-slice
  71.7 0.0 copy-done.2
  71.7 0.3 select_reduce_fusion.1
  72.0 0.2 convert_reduce_fusion.1
  72.2 7.8 %all-to-all-done.1 = f32[8,1,32,512]{3,2,1,0:T(8,128)S(1)} async-done(((f32[8,1,32,512]{3,2,1,0:T(8,128)}), f32[8,1,32,512]{3,2,1,0:T(8,128)S(1)}, u32[]{:S(2)}, u32[]{:S(2)}) %all-to-all-start.1) | async-done | bytes 524320 | tf_op jit(solution)/shard_map/all_to_all | solution.py:73
  80.0 0.1 multiply_reduce_fusion
  80.1 0.2 fusion.9
  80.3 3.5 %fusion.16 = f32[32,1,128]{2,1,0:T(1,128)S(1)} fusion(bf16[32,512,128]{2,1,0:T(8,128)(2,1)} %param.13, f32[32,512,1]{1,0,2:T(8,128)S(1)} %fusion.9), kind=kOutput, calls=%fused_computation.22 | convolution fusion | flops 25165824 | bytes 4276224 | tf_op jit(solution)/shard_map/rhc,hcv->rhv/dot_general | solution.py:22
  83.9 30.5 %all-gather = bf16[8,1,4096]{2,1,0:T(2,128)(2,1)S(1)} all-gather(bf16[1,1,4096]{2,1,0:T(2,128)(2,1)S(1)} %reshape.166), channel_id=1, replica_groups=mesh['ctx'=8,'tp'=4] {'ctx'}, dimensions={0}, use_global_device_ids=true | all-gather | bytes 73728 | tf_op jit(solution)/shard_map/all_gather | solution.py:86
  114.4 4.1 %fusion.13 = f32[8,896]{1,0:T(8,128)S(1)} fusion(bf16[4096,896]{1,0:T(8,128)(2,1)} %param.14, bf16[8,1,4096]{2,1,0:T(2,128)(2,1)S(1)} %all-gather), kind=kOutput, calls=%fused_computation.18 | convolution fusion | flops 58720256 | bytes 7434240 | tf_op jit(solution)/shard_map/dot_general | solution.py:88
  118.6 10.3 %all-reduce = bf16[8,896]{1,0:T(8,128)(2,1)S(1)} all-reduce(f32[8,896]{1,0:T(8,128)S(1)} %fusion.13), channel_id=2, replica_groups=mesh['ctx'=8,'tp'=4] {'tp'}, use_global_device_ids=true, to_apply=%region_7.8.clone | all-reduce | flops 7168 | bytes 43008
  128.9 0.6 dynamic-slice_convert_fusion
  (9 shorter events, 0.1 us)
Async XLA Ops:
  0.0 0.9 copy-start
  0.0 3.9 %copy-start.3 = (bf16[1,32,64]{2,1,0:T(8,128)(2,1)S(1)}, bf16[1,32,64]{2,1,0:T(8,128)(2,1)}, u32[]{:S(2)}) copy-start(bf16[1,32,64]{2,1,0:T(8,128)(2,1)} %param.11) | copy-start | bytes 12292
  0.0 36.6 %copy-start.4 = (s32[8]{0:T(128)S(1)}, s32[8]{0:T(128)}, u32[]{:S(2)}) copy-start(s32[8]{0:T(128)} %param.17) | copy-start | bytes 100
  0.9 35.8 %copy-start.5 = (bf16[4096,576]{0,1:T(8,128)(2,1)S(1)}, bf16[4096,576]{0,1:T(8,128)(2,1)}, u32[]{:S(2)}) copy-start(bf16[4096,576]{0,1:T(8,128)(2,1)} %param.15) | copy-start | bytes 14155780
  39.4 1.9 %copy-start.1 = (f32[8,32,4096]{2,1,0:T(8,128)}, f32[8,32,4096]{2,1,0:T(8,128)S(1)}, u32[]{:S(2)}) copy-start(f32[8,32,4096]{2,1,0:T(8,128)S(1)} %get-tuple-element.10) | copy-start | bytes 12582916
  54.9 9.7 %all-to-all-start = ((f32[8,1,32]{2,1,0:T(1,128)}), f32[8,1,32]{2,1,0:T(1,128)S(1)}, u32[]{:S(2)}, u32[]{:S(2)}) async-start(f32[8,1,32]{2,1,0:T(1,128)} %bitcast.5), calls=%async_computation | async-start | bytes 8192 | tf_op jit(solution)/shard_map/all_to_all | solution.py:71
  58.1 12.2 %copy-start.6 = (u32[32]{0:T(128)S(1)}, u32[32]{0:T(128)}, u32[]{:S(2)}) copy-start(u32[32]{0:T(128)} %constant.17) | copy-start | bytes 388
  58.1 13.6 %copy-start.2 = (bf16[1,256,576]{1,2,0:T(8,128)(2,1)S(1)}, bf16[1,256,576]{1,2,0:T(8,128)(2,1)}, u32[]{:S(2)}) copy-start(bf16[1,256,576]{1,2,0:T(8,128)(2,1)} %param.18) | copy-start | bytes 884740
  64.5 15.5 %all-to-all-start.1 = ((f32[8,1,32,512]{3,2,1,0:T(8,128)}), f32[8,1,32,512]{3,2,1,0:T(8,128)S(1)}, u32[]{:S(2)}, u32[]{:S(2)}) async-start(f32[8,1,32,512]{3,2,1,0:T(8,128)} %fusion.4), calls=%async_computation.1 | async-start | bytes 1048576 | tf_op jit(solution)/shard_map/all_to_all | solution.py:73
where the time goes:
time: 130 us; the launch traced here: 129 us
  blocking collectives  85.4 us (66%)
  matrix products  19.4 us (15%)
  waiting for transfers between devices  8.58 us (7%)
  starting transfers between devices  8.34 us (6%)
  local copies, waits for them, and re-layouts  3.31 us (3%)
  other arithmetic  3 us (2%)
  between operations  1.49 us (1%)
    all_gather x1, blocking collectives, on_device(): all_queries = lax.all_gather(own_queries, 'ctx', axis=0, tiled=True)  32.7 us
    all_gather x1, blocking collectives, on_device(): every_value = lax.all_gather(flat_values, 'ctx', axis=0, tiled=True)  30.5 us
    all_to_all x1, blocking collectives, on_device(): lax.all_to_all(by_owner(row_mass), 'ctx', split_axis=0, concat_axis=0, ti...  11.8 us
    unnamed x1, blocking collectives  10.3 us
    all_to_all x1, waiting for transfers between devices, on_device(): lax.all_to_all(by_owner(row_weighted), 'ctx', split_axis=0, concat_axis=0...  7.78 us
    dot_general x2, matrix products, partial_stats(): jnp.einsum(pattern, weights, values, preferred_element_type=jnp.float32)  5.81 us
    all_to_all x1, starting transfers between devices, on_device(): lax.all_to_all(by_owner(row_weighted), 'ctx', split_axis=0, concat_axis=0...  5.12 us
    dot_general x1, matrix products, on_device(): jnp.dot(every_value, w_out, preferred_element_type=jnp.float32)  4.14 us
  transfers between devices with their start and end apart: 2, of which 2 were waited for; matrix products, arithmetic and copies ran while one was open for 5% of the time, Pallas kernels for 0%

commit v1 on v0

--- a/solution.py
+++ b/solution.py
@@ -8,6 +8,20 @@
 NOPE = 128
 BLOCK = 64
 masked_value = -1e30
+
+
+def work_both_ways(array, axis, dim, make, out_dim):
+    ways, here, step = (lax.axis_size(axis), lax.axis_index(axis), array.shape[dim])
+    earlier, later = ([], [])
+    going_up = going_down = array
+    for far in range(ways // 2 + 1):
+        earlier.append(make(going_up, (here - far) % ways * step))
+        if 0 < far < ways - ways // 2:
+            later.append(make(going_down, (here + far) % ways * step))
+        going_up = lax.ppermute(going_up, axis, [(d, (d + 1) % ways) for d in range(ways)])
+        going_down = lax.ppermute(going_down, axis, [(d, (d - 1) % ways) for d in range(ways)])
+    line = jnp.concatenate([*earlier[::-1], *later], axis=out_dim)
+    return jnp.roll(line, (here - ways // 2) * earlier[0].shape[out_dim], axis=out_dim)
 
 
 def partial_stats(scores, visible, values, pattern):
@@ -39,7 +53,6 @@
         jnp.bfloat16
     )
     own_queries = jnp.concatenate([q_latent, q_rope], axis=2)
-    all_queries = lax.all_gather(own_queries, "ctx", axis=0, tiled=True)
     ctx_count = lax.axis_size("ctx")
     own_count = own_queries.shape[0]
     value_weight = w_uv.astype(jnp.float32)
@@ -48,7 +61,15 @@
     ).reshape(-1)
     visible = (positions[None, :] < prefix_len[:, None])[:, None, :]
     scores = (
-        jnp.einsum("rhc,tc->rht", all_queries, prefix_cache, preferred_element_type=jnp.float32)
+        work_both_ways(
+            own_queries,
+            "ctx",
+            0,
+            lambda own_block, offset: jnp.einsum(
+                "rhc,tc->rht", own_block, prefix_cache, preferred_element_type=jnp.float32
+            ),
+            0,
+        )
         * softmax_scale
     )
     row_peak, row_mass, row_weighted = partial_stats(

time: 130 us -> 132 us (1.015)
  blocking collectives: 85.4 us -> 49.7 us
  starting transfers between devices: 8.34 us -> 24 us
  waiting for transfers between devices: 8.58 us -> 19.5 us
  matrix products: 19.4 us -> 26.3 us
  other arithmetic: 3 us -> 6.28 us
    all_gather x1 -> x0, blocking collectives: 32.7 us -> none  [on_device(): all_queries = lax.all_gather(own_queries, 'ctx', axis=0, tiled=True)]
    ppermute x0 -> x7, starting transfers between devices: none -> 15.6 us  [the longest x3 12.6 us: work_both_ways(): lax.ppermute(going_down, axis, [(d, (d - 1) % ways) for d in range(ways)])]
    ppermute x0 -> x7, waiting for transfers between devices: none -> 10.9 us  [the longest x4 10.9 us: work_both_ways(): lax.ppermute(going_up, axis, [(d, (d + 1) % ways) for d in range(ways)])]
    dot_general x1 -> x8, matrix products: 2.69 us -> 9.7 us  [on_device(): jnp.einsum('rhc,tc->rht', own_block, prefix_cache, preferred_element_type...]
    all_to_all x1, blocking collectives: 11.8 us -> 8.85 us  [on_device(): lax.all_to_all(by_owner(row_mass), 'ctx', split_axis=0, concat_axis=0, ti...]
    reduce_max x0 -> x1, other arithmetic: none -> 1.84 us  [partial_stats(): row_peak = jnp.max(jnp.where(visible, scores, masked_value), axis=2)]
    unnamed x16 -> x21, local copies, waits for them, and re-layouts: 2.63 us -> 2.98 us
  transfers between devices with their start and end apart: 2 -> 9, of which waited for: 2 -> 6; matrix products, arithmetic and copies ran while one was open for 5% -> 13% of each run, Pallas kernels for 0% -> 0%
where the time goes in v1:
time: 132 us; the launch traced here: 131 us
  blocking collectives  49.7 us (38%)
  matrix products  26.3 us (20%)
  starting transfers between devices  24 us (18%)
  waiting for transfers between devices  19.5 us (15%)
  other arithmetic  6.28 us (5%)
  local copies, waits for them, and re-layouts  3.7 us (3%)
  between operations  1.55 us (1%)
    all_gather x1, blocking collectives, on_device(): every_value = lax.all_gather(flat_values, 'ctx', axis=0, tiled=True)  30.5 us
    ppermute x3, starting transfers between devices, work_both_ways(): lax.ppermute(going_down, axis, [(d, (d - 1) % ways) for d in range(ways)])  12.6 us
    ppermute x4, waiting for transfers between devices, work_both_ways(): lax.ppermute(going_up, axis, [(d, (d + 1) % ways) for d in range(ways)])  10.9 us
    unnamed x1, blocking collectives  10.3 us
    dot_general x8, matrix products, on_device(): jnp.einsum('rhc,tc->rht', own_block, prefix_cache, preferred_element_type...  9.7 us
    all_to_all x1, blocking collectives, on_device(): lax.all_to_all(by_owner(row_mass), 'ctx', split_axis=0, concat_axis=0, ti...  8.85 us
    all_to_all x1, waiting for transfers between devices, on_device(): lax.all_to_all(by_owner(row_weighted), 'ctx', split_axis=0, concat_axis=0...  7.83 us
    dot_general x2, matrix products, partial_stats(): jnp.einsum(pattern, weights, values, preferred_element_type=jnp.float32)  5.87 us
  transfers between devices with their start and end apart: 9, of which 6 were waited for; matrix products, arithmetic and copies ran while one was open for 13% of the time, Pallas kernels for 0%

profile of v1, /device:TPU:0, one launch (start us, length us, event | category | flops | bytes accessed | tf_op | source)
XLA Modules:
  0.0 131.0 jit_solution(7794038126521634561)
XLA Ops:
  0.0 0.0 copy-start
  0.0 0.7 copy-done
  0.7 2.8 %fusion.27 = bf16[32,1,512]{2,1,0:T(2,128)(2,1)S(1)} fusion(bf16[32,128,512]{2,1,0:T(8,128)(2,1)} %param.12, bf16[32,128,1]{1,0,2:T(8,128)(2,1)S(1)} %bitcast.112), kind=kOutput, calls=%fused_computation.63 | convolution fusion | flops 4194304 | bytes 4235264 | tf_op jit(solution)/shard_map/rhn,hnc->rhc/dot_general | solution.py:52
  3.6 0.7 pad_maximum_fusion
  4.3 3.0 %collective-permute-start = (bf16[1,32,576]{2,1,0:T(8,128)(2,1)S(1)}, bf16[1,32,576]{2,1,0:T(8,128)(2,1)S(1)}, u32[]{:S(2)}, u32[]{:S(2)}) collective-permute-start(bf16[1,32,576]{2,1,0:T(8,128)(2,1)S(1)} %pad_maximum_fusion), channel_id=1, source_target_pairs={{0,4},{4,8},{8,12},{12,16},{16,20},{20,24},{24,28},{28,0},{1,5},{5... | collective-permute-start | bytes 110600 | tf_op jit(solution)/shard_map/ppermute | solution.py:21
  7.2 3.1 %collective-permute-start.4 = (bf16[1,32,576]{2,1,0:T(8,128)(2,1)S(1)}, bf16[1,32,576]{2,1,0:T(8,128)(2,1)S(1)}, u32[]{:S(2)}, u32[]{:S(2)}) collective-permute-start(bf16[1,32,576]{2,1,0:T(8,128)(2,1)S(1)} %pad_maximum_fusion), channel_id=1, source_target_pairs={{0,28},{4,0},{8,4},{12,8},{16,12},{20,16},{24,20},{28,24},{1,29},{... | collective-permute-start | bytes 110600 | tf_op jit(solution)/shard_map/ppermute | solution.py:22
  10.3 1.9 %collective-permute-done = bf16[1,32,576]{2,1,0:T(8,128)(2,1)S(1)} collective-permute-done((bf16[1,32,576]{2,1,0:T(8,128)(2,1)S(1)}, bf16[1,32,576]{2,1,0:T(8,128)(2,1)S(1)}, u32[]{:S(2)}, u32[]{:S(2)}) %collective-permute-start) | collective-permute-done | bytes 36896 | tf_op jit(solution)/shard_map/ppermute | solution.py:21
  12.2 0.0 collective-permute-start.1
  12.2 0.7 broadcast_multiply_fusion
  12.9 6.0 %collective-permute-done.1 = bf16[1,32,576]{2,1,0:T(8,128)(2,1)S(1)} collective-permute-done((bf16[1,32,576]{2,1,0:T(8,128)(2,1)S(1)}, bf16[1,32,576]{2,1,0:T(8,128)(2,1)S(1)}, u32[]{:S(2)}, u32[]{:S(2)}) %collective-permute-start.1) | collective-permute-done | bytes 36896 | tf_op jit(solution)/shard_map/ppermute | solution.py:21
  18.9 0.0 collective-permute-start.2
  18.9 0.1 iota_add_fusion
  19.0 0.1 add.49
  19.1 0.0 collective-permute-done.4
  19.1 4.7 %collective-permute-start.5 = (bf16[1,32,576]{2,1,0:T(8,128)(2,1)S(1)}, bf16[1,32,576]{2,1,0:T(8,128)(2,1)S(1)}, u32[]{:S(2)}, u32[]{:S(2)}) collective-permute-start(bf16[1,32,576]{2,1,0:T(8,128)(2,1)S(1)} %collective-permute-done.4), channel_id=1, source_target_pairs={{0,28},{4,0},{8,4},{12,8},{16,12},{20,16},{24,20},{28,24},{1,29},{... | collective-permute-start | bytes 110600 | tf_op jit(solution)/shard_map/ppermute | solution.py:22
  23.8 1.8 %collective-permute-done.2 = bf16[1,32,576]{2,1,0:T(8,128)(2,1)S(1)} collective-permute-done((bf16[1,32,576]{2,1,0:T(8,128)(2,1)S(1)}, bf16[1,32,576]{2,1,0:T(8,128)(2,1)S(1)}, u32[]{:S(2)}, u32[]{:S(2)}) %collective-permute-start.2) | collective-permute-done | bytes 36896 | tf_op jit(solution)/shard_map/ppermute | solution.py:21
  25.6 0.0 collective-permute-start.3
  25.6 0.7 broadcast_compare_fusion
  26.4 0.0 copy-start.1
  26.4 0.0 collective-permute-done.5
  26.4 4.8 %collective-permute-start.6 = (bf16[1,32,576]{2,1,0:T(8,128)(2,1)S(1)}, bf16[1,32,576]{2,1,0:T(8,128)(2,1)S(1)}, u32[]{:S(2)}, u32[]{:S(2)}) collective-permute-start(bf16[1,32,576]{2,1,0:T(8,128)(2,1)S(1)} %collective-permute-done.5), channel_id=1, source_target_pairs={{0,28},{4,0},{8,4},{12,8},{16,12},{20,16},{24,20},{28,24},{1,29},{... | collective-permute-start | bytes 110600 | tf_op jit(solution)/shard_map/ppermute | solution.py:22
  31.2 1.1 collective-permute-done.3
  32.3 3.2 %constant_dynamic-update-slice_fusion.15 = (f32[16,32,4096]{2,1,0:T(8,128)S(1)}, f32[1,32,4096]{2,1,0:T(8,128)S(1)}) fusion(bf16[4096,576]{0,1:T(8,128)(2,1)} %param.15, bf16[1,32,576]{2,1,0:T(8,128)(2,1)S(1)} %collective-permute-done.3), kind=kOutput, calls=%fused_computation.57 | convolution fusion | flops 150994944 | bytes 5804032 | tf_op jit(solution)/shard_map/rhc,tc->rht/dot_general | solution.py:68
  35.6 0.0 copy-done.1
  35.6 0.9 constant_dynamic-update-slice_fusion.14
  36.5 0.0 copy-start.4
  36.5 0.9 constant_dynamic-update-slice_fusion.13
  37.5 0.9 constant_dynamic-update-slice_fusion.12
  38.4 0.0 copy-done.4
  38.4 0.9 constant_dynamic-update-slice_fusion.11
  39.3 0.9 constant_dynamic-update-slice_fusion.10
  40.3 0.9 constant_dynamic-update-slice_fusion.9
  41.2 0.0 collective-permute-done.6
  41.2 0.9 constant_dynamic-update-slice_fusion.8
  42.1 0.1 constant_dynamic-update-slice_fusion.7
  42.5 0.0 copy-start.2
  42.5 1.8 %select_reduce_fusion = f32[8,32]{1,0:T(8,128)} fusion(f32[16,32,4096]{2,1,0:T(8,128)S(1)} %constant_dynamic-update-slice_fusion, s32[]{:T(128)S(6)} %select_n.30, pred[8,4096]{1,0:T(8,128)(4,1)S(1)} %broadcast_compare_fusion), kind=kLoop, calls=%fused_computation.13 | loop fusion | flops 3145472 | bytes 4228100 | tf_op jit(solution)/shard_map/reduce_max | solution.py:28
  44.3 1.4 %copy-done.2 = f32[16,32,4096]{2,1,0:T(8,128)} copy-done((f32[16,32,4096]{2,1,0:T(8,128)}, f32[16,32,4096]{2,1,0:T(8,128)S(1)}, u32[]{:S(2)}) %copy-start.2) | copy-done | bytes 8388632
  45.7 1.9 %convert_reduce_fusion = f32[8,32]{1,0:T(8,128)S(1)} fusion(f32[8,32]{1,0:T(8,128)} %select_reduce_fusion, f32[16,32,4096]{2,1,0:T(8,128)S(1)} %constant_dynamic-update-slice_fusion, s32[]{:T(128)S(6)} %select_n.30, pred[8,4096]{1,0:T(8,128)(4,1)S(1)} %broadcast_compare_fusion), kind=kLoop, calls=%fused_computation.10 | loop fusion | flops 6291200 | bytes 4229124 | tf_op jit(solution)/shard_map/reduce_sum | solution.py:30
  47.6 8.8 %all_to_all.15 = f32[8,1,32]{2,1,0:T(1,128)S(1)} all-to-all(f32[8,1,32]{2,1,0:T(1,128)S(1)} %bitcast.118), channel_id=1, replica_groups=mesh['ctx'=8,'tp'=4] {'ctx'}, dimensions={0} | all-to-all | bytes 2048 | tf_op jit(solution)/shard_map/all_to_all | solution.py:93
  56.4 3.2 %all-to-all-start = ((f32[8,1,32]{2,1,0:T(1,128)}), f32[8,1,32]{2,1,0:T(1,128)S(1)}, u32[]{:S(2)}, u32[]{:S(2)}) async-start(f32[8,1,32]{2,1,0:T(1,128)} %bitcast.20), calls=%async_computation | async-start | bytes 8192 | tf_op jit(solution)/shard_map/all_to_all | solution.py:92
  59.7 0.0 copy-start.5
  59.7 0.0 copy-start.3
  59.7 5.7 %fusion.3 = f32[8,1,32,512]{3,2,1,0:T(8,128)} fusion(bf16[4096,576]{0,1:T(8,128)(2,1)} %param.15, f32[16,32,4096]{2,1,0:T(8,128)} %copy-done.2, s32[]{:T(128)S(6)} %select_n.30, f32[8,32]{1,0:T(8,128)} %select_reduce_fusion, pred[8,4096]{1,0:T(8,128)(4,1)S(1)} %broadcast_compare_fusion), kind=kOutput, calls=%fused_computation.15 | convolution fusion | flops 1077936128 | bytes 8949764 | tf_op jit(solution)/shard_map/rht,tc->rhc/dot_general | solution.py:31
  65.4 0.7 all-to-all-done
  66.1 5.2 %all-to-all-start.1 = ((f32[8,1,32,512]{3,2,1,0:T(8,128)}), f32[8,1,32,512]{3,2,1,0:T(8,128)S(1)}, u32[]{:S(2)}, u32[]{:S(2)}) async-start(f32[8,1,32,512]{3,2,1,0:T(8,128)} %fusion.3), calls=%async_computation.1 | async-start | bytes 1048576 | tf_op jit(solution)/shard_map/all_to_all | solution.py:94
  71.9 0.0 copy-done.5
  71.9 0.6 dynamic-slice
  73.2 0.0 copy-done.3
  73.2 0.3 select_reduce_fusion.1
  73.4 0.2 convert_reduce_fusion.1
  73.7 7.8 %all-to-all-done.1 = f32[8,1,32,512]{3,2,1,0:T(8,128)S(1)} async-done(((f32[8,1,32,512]{3,2,1,0:T(8,128)}), f32[8,1,32,512]{3,2,1,0:T(8,128)S(1)}, u32[]{:S(2)}, u32[]{:S(2)}) %all-to-all-start.1) | async-done | bytes 524320 | tf_op jit(solution)/shard_map/all_to_all | solution.py:94
  81.6 0.1 multiply_reduce_fusion
  81.7 0.2 fusion.8
  81.9 3.5 %fusion.15 = f32[32,1,128]{2,1,0:T(1,128)S(1)} fusion(bf16[32,512,128]{2,1,0:T(8,128)(2,1)} %param.13, f32[32,512,1]{1,0,2:T(8,128)S(1)} %fusion.8), kind=kOutput, calls=%fused_computation.29 | convolution fusion | flops 25165824 | bytes 4276224 | tf_op jit(solution)/shard_map/rhc,hcv->rhv/dot_general | solution.py:36
  85.4 30.5 %all-gather = bf16[8,1,4096]{2,1,0:T(2,128)(2,1)S(1)} all-gather(bf16[1,1,4096]{2,1,0:T(2,128)(2,1)S(1)} %reshape.203), channel_id=1, replica_groups=mesh['ctx'=8,'tp'=4] {'ctx'}, dimensions={0}, use_global_device_ids=true | all-gather | bytes 73728 | tf_op jit(solution)/shard_map/all_gather | solution.py:107
  115.9 4.1 %fusion.12 = f32[8,896]{1,0:T(8,128)S(1)} fusion(bf16[4096,896]{1,0:T(8,128)(2,1)} %param.14, bf16[8,1,4096]{2,1,0:T(2,128)(2,1)S(1)} %all-gather), kind=kOutput, calls=%fused_computation.25 | convolution fusion | flops 58720256 | bytes 7434240 | tf_op jit(solution)/shard_map/dot_general | solution.py:109
  120.1 10.3 %all-reduce = bf16[8,896]{1,0:T(8,128)(2,1)S(1)} all-reduce(f32[8,896]{1,0:T(8,128)S(1)} %fusion.12), channel_id=2, replica_groups=mesh['ctx'=8,'tp'=4] {'tp'}, use_global_device_ids=true, to_apply=%region_7.8.clone | all-reduce | flops 7168 | bytes 43008
  130.4 0.6 dynamic-slice_convert_fusion
  (15 shorter events, 0.4 us)
Async XLA Ops:
  0.0 0.7 copy-start
  4.3 8.0 %collective-permute-start = (bf16[1,32,576]{2,1,0:T(8,128)(2,1)S(1)}, bf16[1,32,576]{2,1,0:T(8,128)(2,1)S(1)}, u32[]{:S(2)}, u32[]{:S(2)}) collective-permute-start(bf16[1,32,576]{2,1,0:T(8,128)(2,1)S(1)} %pad_maximum_fusion), channel_id=1, source_target_pairs={{0,4},{4,8},{8,12},{12,16},{16,20},{20,24},{24,28},{28,0},{1,5},{5... | collective-permute-start | bytes 110600 | tf_op jit(solution)/shard_map/ppermute | solution.py:21
  7.2 11.9 %collective-permute-start.4 = (bf16[1,32,576]{2,1,0:T(8,128)(2,1)S(1)}, bf16[1,32,576]{2,1,0:T(8,128)(2,1)S(1)}, u32[]{:S(2)}, u32[]{:S(2)}) collective-permute-start(bf16[1,32,576]{2,1,0:T(8,128)(2,1)S(1)} %pad_maximum_fusion), channel_id=1, source_target_pairs={{0,28},{4,0},{8,4},{12,8},{16,12},{20,16},{24,20},{28,24},{1,29},{... | collective-permute-start | bytes 110600 | tf_op jit(solution)/shard_map/ppermute | solution.py:22
  12.2 6.7 %collective-permute-start.1 = (bf16[1,32,576]{2,1,0:T(8,128)(2,1)S(1)}, bf16[1,32,576]{2,1,0:T(8,128)(2,1)S(1)}, u32[]{:S(2)}, u32[]{:S(2)}) collective-permute-start(bf16[1,32,576]{2,1,0:T(8,128)(2,1)S(1)} %collective-permute-done), channel_id=1, source_target_pairs={{0,4},{4,8},{8,12},{12,16},{16,20},{20,24},{24,28},{28,0},{1,5},{5... | collective-permute-start | bytes 110600 | tf_op jit(solution)/shard_map/ppermute | solution.py:21
  18.9 6.7 %collective-permute-start.2 = (bf16[1,32,576]{2,1,0:T(8,128)(2,1)S(1)}, bf16[1,32,576]{2,1,0:T(8,128)(2,1)S(1)}, u32[]{:S(2)}, u32[]{:S(2)}) collective-permute-start(bf16[1,32,576]{2,1,0:T(8,128)(2,1)S(1)} %collective-permute-done.1), channel_id=1, source_target_pairs={{0,4},{4,8},{8,12},{12,16},{16,20},{20,24},{24,28},{28,0},{1,5},{5... | collective-permute-start | bytes 110600 | tf_op jit(solution)/shard_map/ppermute | solution.py:21
  19.1 7.3 %collective-permute-start.5 = (bf16[1,32,576]{2,1,0:T(8,128)(2,1)S(1)}, bf16[1,32,576]{2,1,0:T(8,128)(2,1)S(1)}, u32[]{:S(2)}, u32[]{:S(2)}) collective-permute-start(bf16[1,32,576]{2,1,0:T(8,128)(2,1)S(1)} %collective-permute-done.4), channel_id=1, source_target_pairs={{0,28},{4,0},{8,4},{12,8},{16,12},{20,16},{24,20},{28,24},{1,29},{... | collective-permute-start | bytes 110600 | tf_op jit(solution)/shard_map/ppermute | solution.py:22
  25.6 6.7 %collective-permute-start.3 = (bf16[1,32,576]{2,1,0:T(8,128)(2,1)S(1)}, bf16[1,32,576]{2,1,0:T(8,128)(2,1)S(1)}, u32[]{:S(2)}, u32[]{:S(2)}) collective-permute-start(bf16[1,32,576]{2,1,0:T(8,128)(2,1)S(1)} %collective-permute-done.2), channel_id=1, source_target_pairs={{0,4},{4,8},{8,12},{12,16},{16,20},{20,24},{24,28},{28,0},{1,5},{5... | collective-permute-start | bytes 110600 | tf_op jit(solution)/shard_map/ppermute | solution.py:21
  26.4 9.2 %copy-start.1 = (bf16[4096,576]{0,1:T(8,128)(2,1)S(1)}, bf16[4096,576]{0,1:T(8,128)(2,1)}, u32[]{:S(2)}) copy-start(bf16[4096,576]{0,1:T(8,128)(2,1)} %param.15) | copy-start | bytes 14155780
  26.4 14.8 %collective-permute-start.6 = (bf16[1,32,576]{2,1,0:T(8,128)(2,1)S(1)}, bf16[1,32,576]{2,1,0:T(8,128)(2,1)S(1)}, u32[]{:S(2)}, u32[]{:S(2)}) collective-permute-start(bf16[1,32,576]{2,1,0:T(8,128)(2,1)S(1)} %collective-permute-done.5), channel_id=1, source_target_pairs={{0,28},{4,0},{8,4},{12,8},{16,12},{20,16},{24,20},{28,24},{1,29},{... | collective-permute-start | bytes 110600 | tf_op jit(solution)/shard_map/ppermute | solution.py:22
  36.5 1.9 %copy-start.4 = (bf16[1,32,64]{2,1,0:T(8,128)(2,1)S(1)}, bf16[1,32,64]{2,1,0:T(8,128)(2,1)}, u32[]{:S(2)}) copy-start(bf16[1,32,64]{2,1,0:T(8,128)(2,1)} %param.11) | copy-start | bytes 12292
  42.5 3.2 %copy-start.2 = (f32[16,32,4096]{2,1,0:T(8,128)}, f32[16,32,4096]{2,1,0:T(8,128)S(1)}, u32[]{:S(2)}) copy-start(f32[16,32,4096]{2,1,0:T(8,128)S(1)} %constant_dynamic-update-slice_fusion) | copy-start | bytes 25165828
  56.4 9.7 %all-to-all-start = ((f32[8,1,32]{2,1,0:T(1,128)}), f32[8,1,32]{2,1,0:T(1,128)S(1)}, u32[]{:S(2)}, u32[]{:S(2)}) async-start(f32[8,1,32]{2,1,0:T(1,128)} %bitcast.20), calls=%async_computation | async-start | bytes 8192 | tf_op jit(solution)/shard_map/all_to_all | solution.py:92
  59.7 12.3 %copy-start.5 = (u32[32]{0:T(128)S(1)}, u32[32]{0:T(128)}, u32[]{:S(2)}) copy-start(u32[32]{0:T(128)} %constant.48) | copy-start | bytes 388
  59.7 13.5 %copy-start.3 = (bf16[1,256,576]{1,2,0:T(8,128)(2,1)S(1)}, bf16[1,256,576]{1,2,0:T(8,128)(2,1)}, u32[]{:S(2)}) copy-start(bf16[1,256,576]{1,2,0:T(8,128)(2,1)} %param.18) | copy-start | bytes 884740
  66.1 15.5 %all-to-all-start.1 = ((f32[8,1,32,512]{3,2,1,0:T(8,128)}), f32[8,1,32,512]{3,2,1,0:T(8,128)S(1)}, u32[]{:S(2)}, u32[]{:S(2)}) async-start(f32[8,1,32,512]{3,2,1,0:T(8,128)} %fusion.3), calls=%async_computation.1 | async-start | bytes 1048576 | tf_op jit(solution)/shard_map/all_to_all | solution.py:94
